TPU v7x, 32 devices: a whole 2x2x4 slice. The times are simulated.
32 devices in a mesh: ctx: 8 (over y, x, core), fsdp: 4 (over z).
Axes of the slice: x: 2, y: 2, z: 4, core: 2. Of those that a mesh axis runs over, the one named last changes fastest.
Arguments:
- tokens: bfloat16 [4, 4096, 768], P('fsdp', 'ctx'), may hold values from -6 to 6
- cotangent: bfloat16 [4, 4096, 768], P('fsdp', 'ctx'), may hold values from -6 to 6
- lengths: int32 [4, 4], P('fsdp'), may hold values from 1 to 2048, 4096 in all within a row
- dealing: int32 [4, 16], P('fsdp'), may hold values from 0 to 15, each once within a row
- qkv_weight: bfloat16 [768, 2304], P('fsdp'), may hold values from -0.21875 to 0.21875
- out_weight: bfloat16 [768, 768], P('fsdp'), may hold values from -0.21875 to 0.21875
- in_weight: bfloat16 [768, 3072], P('fsdp'), may hold values from -0.21875 to 0.21875
- back_weight: bfloat16 [3072, 768], P('fsdp'), may hold values from -0.109375 to 0.109375
- norm_gains: bfloat16 [3, 768], P(None, 'fsdp'), may hold values from 0.25 to 1.75
- shifts: bfloat16 [7, 768], P(None, 'fsdp'), may hold values from -1.796875 to 1.796875
- ffn_gain: bfloat16 [3072], P('fsdp'), may hold values from 0.25 to 1.75
- ffn_shifts: bfloat16 [2, 3072], P(None, 'fsdp'), may hold values from -1.796875 to 1.796875
Outputs:
- mixed_out: bfloat16 [4, 4096, 768], P('fsdp', 'ctx')
- input_grad: float32 [4, 4096, 768], P('fsdp', 'ctx')
- qkv_grad: float32 [768, 2304], P(('ctx', 'fsdp'))
- out_grad: float32 [768, 768], P(('ctx', 'fsdp'))
- in_grad: float32 [768, 3072], P(('ctx', 'fsdp'))
- back_grad: float32 [3072, 768], P(('ctx', 'fsdp'))
- gains_grad: float32 [3, 768], P(None, ('ctx', 'fsdp'))
- shifts_grad: float32 [7, 768], P(None, ('ctx', 'fsdp'))
- ffn_gain_grad: float32 [3072], P(('ctx', 'fsdp'))
- ffn_shifts_grad: float32 [2, 3072], P(None, ('ctx', 'fsdp'))
Inputs may be any that keep to these rules, and one draw needn't show every extreme that they name: `lengths`: each row sums to 4096 and its largest entry is exactly 2048. `dealing`: each row is a permutation of the group numbers.
All inputs are finite; a program needn't handle non-finite values.
Results may differ from a plain program's by a relative error of at most 0.018.
Values may be sent and summed in bfloat16 or wider, within the bound.
No kernel may reach another device: no remote copies, remote signals or barrier semaphores. Data moves between devices by JAX's collectives and lax.ppermute only.
A program may use at most 256 MiB of HBM per device.

v0:
```python
import math
import jax
import jax.numpy as jnp
from jax import lax
from jax.sharding import PartitionSpec as P

D = 768
H = 12
DH = 64


def layer_norm(values, gain, shift):
    average = jnp.mean(values, axis=-1, keepdims=True)
    centred = values - average
    variance = jnp.mean(centred * centred, axis=-1, keepdims=True)
    return centred * lax.rsqrt(variance + 1e-05) * gain + shift


def gelu_exact(values):
    return jax.nn.gelu(values, approximate=False)


def row_places(first_row, row_count, deal_row, bounds, group_rows):
    row_ids = first_row + jnp.arange(row_count, dtype=jnp.int32)
    group_ids = row_ids // group_rows
    onehot = (group_ids[:, None] == jnp.arange(deal_row.shape[0], dtype=jnp.int32)[None, :]).astype(
        jnp.int32
    )
    picked = jnp.sum(onehot * deal_row[None, :], axis=1)
    places = picked * group_rows + row_ids % group_rows
    segment = jnp.sum((places[:, None] >= bounds[None, :]).astype(jnp.int32), axis=1)
    return (places, segment)


def outer_sum(left, right):
    return lax.dot_general(
        left, right, (((0,), (0,)), ((), ())), preferred_element_type=jnp.float32
    )


def times_transposed(left, matrix):
    return lax.dot_general(
        left, matrix, (((1,), (1,)), ((), ())), preferred_element_type=jnp.float32
    )


def unpack(loaded):
    qkv_w, out_w, in_w, back_w, gains, shift_rows, ffn_gain, ffn_shift_rows = loaded
    return (
        qkv_w,
        out_w,
        in_w,
        back_w,
        gains.astype(jnp.float32),
        shift_rows.astype(jnp.float32),
        ffn_gain.astype(jnp.float32),
        ffn_shift_rows.astype(jnp.float32),
    )


def local(
    tokens,
    cotangent,
    lengths,
    dealing,
    qkv_weight,
    out_weight,
    in_weight,
    back_weight,
    norm_gains,
    shifts,
    ffn_gain,
    ffn_shifts,
):
    position = lax.axis_index("ctx")
    tok_rows = tokens.shape[1]
    group_rows = tok_rows // 2
    deal_row = dealing[0]
    bounds = jnp.cumsum(lengths[0])
    scaling = DH ** (-0.5)
    loaded = (
        lax.all_gather(qkv_weight, "fsdp", axis=0, tiled=True),
        lax.all_gather(out_weight, "fsdp", axis=0, tiled=True),
        lax.all_gather(in_weight, "fsdp", axis=0, tiled=True),
        lax.all_gather(back_weight, "fsdp", axis=0, tiled=True),
        lax.all_gather(norm_gains, "fsdp", axis=1, tiled=True),
        lax.all_gather(shifts, "fsdp", axis=1, tiled=True),
        lax.all_gather(ffn_gain, "fsdp", axis=0, tiled=True),
        lax.all_gather(ffn_shifts, "fsdp", axis=1, tiled=True),
    )
    qkv_w, out_w, in_w, back_w, gains, shift_rows, ffn_scale, ffn_shift_rows = unpack(loaded)
    inputs = tokens[0].astype(jnp.float32)
    normed = layer_norm(inputs, gains[0], shift_rows[0])
    normed_low = normed.astype(jnp.bfloat16)
    projected = jnp.dot(normed_low, qkv_w, preferred_element_type=jnp.float32)
    query = (projected[:, :D] + shift_rows[1]).astype(jnp.bfloat16)
    keyed = projected[:, D : 2 * D].astype(jnp.bfloat16)
    valued = (projected[:, 2 * D :] + shift_rows[2]).astype(jnp.bfloat16)
    query3 = query.reshape(tok_rows, H, DH)
    q_places, q_segment = row_places(position * tok_rows, tok_rows, deal_row, bounds, group_rows)

    def allowed_pairs(qp, qs, k_places, k_segment):
        return ((k_segment[None, :] == qs[:, None]) & (k_places[None, :] <= qp[:, None]))[None]

    initial = (
        jnp.full((H, tok_rows), -1e30, jnp.float32),
        jnp.zeros((H, tok_rows), jnp.float32),
        jnp.zeros((H, tok_rows, DH), jnp.float32),
    )
    key_rows = lax.all_gather(keyed, "ctx", axis=0, tiled=True)
    value_rows = lax.all_gather(valued, "ctx", axis=0, tiled=True)
    key_count = key_rows.shape[0]
    block_rows = 512
    block_count = key_count // block_rows
    k_places, k_segment = row_places(jnp.int32(0), key_count, deal_row, bounds, group_rows)
    stacked = (
        key_rows.reshape(block_count, block_rows, H, DH),
        value_rows.reshape(block_count, block_rows, H, DH),
        k_places.reshape(block_count, block_rows),
        k_segment.reshape(block_count, block_rows),
    )

    def visit_block(inner_state, pieces):
        maxima, totals, weighted = inner_state
        key3, value3, block_places, block_segment = pieces
        scores = (
            jnp.einsum("qhd,khd->hqk", query3, key3, preferred_element_type=jnp.float32) * scaling
        )
        allowed = allowed_pairs(q_places, q_segment, block_places, block_segment)
        masked = jnp.where(allowed, scores, -1e30)
        raised = jnp.maximum(maxima, jnp.max(masked, axis=-1))
        rescale = jnp.exp(maxima - raised)
        expo = jnp.where(allowed, jnp.exp(masked - raised[..., None]), 0.0)
        totals = totals * rescale + jnp.sum(expo, axis=-1)
        weighted = weighted * rescale[..., None] + jnp.einsum(
            "hqk,khd->hqd", expo.astype(jnp.bfloat16), value3, preferred_element_type=jnp.float32
        )
        return ((raised, totals, weighted), None)

    maxima, totals, weighted = lax.scan(visit_block, initial, stacked)[0]
    context3 = weighted / totals[..., None]
    log_total = maxima + jnp.log(totals)
    context = context3.transpose(1, 0, 2).reshape(tok_rows, D)
    inner = layer_norm(context, gains[1], shift_rows[3])
    inner_low = inner.astype(jnp.bfloat16)
    branch = jnp.dot(inner_low, out_w, preferred_element_type=jnp.float32) + shift_rows[4]
    middle = inputs + branch
    normed_two = layer_norm(middle, gains[2], shift_rows[5])
    normed_two_low = normed_two.astype(jnp.bfloat16)
    hidden = jnp.dot(normed_two_low, in_w, preferred_element_type=jnp.float32) + ffn_shift_rows[0]
    activated = gelu_exact(hidden)
    inner_two = layer_norm(activated, ffn_scale, ffn_shift_rows[1])
    inner_two_low = inner_two.astype(jnp.bfloat16)
    result = jnp.dot(inner_two_low, back_w, preferred_element_type=jnp.float32) + shift_rows[6]
    mixed_out = (middle + result).astype(jnp.bfloat16)
    loaded_back = (
        lax.all_gather(qkv_weight, "fsdp", axis=0, tiled=True),
        lax.all_gather(out_weight, "fsdp", axis=0, tiled=True),
        lax.all_gather(in_weight, "fsdp", axis=0, tiled=True),
        lax.all_gather(back_weight, "fsdp", axis=0, tiled=True),
        lax.all_gather(norm_gains, "fsdp", axis=1, tiled=True),
        lax.all_gather(shifts, "fsdp", axis=1, tiled=True),
        lax.all_gather(ffn_gain, "fsdp", axis=0, tiled=True),
        lax.all_gather(ffn_shifts, "fsdp", axis=1, tiled=True),
    )
    qkv_w, out_w, in_w, back_w, gains, shift_rows, ffn_scale, ffn_shift_rows = unpack(loaded_back)
    upstream = cotangent[0].astype(jnp.float32)
    result_low = cotangent[0]
    grad_back_w = outer_sum(inner_two_low, result_low)
    grad_back_bias = jnp.sum(result_low.astype(jnp.float32), axis=0)
    grad_inner_two = times_transposed(result_low, back_w)
    norm_pull = jax.vjp(layer_norm, activated, ffn_scale, ffn_shift_rows[1])[1]
    grad_activated, grad_ffn_gain, grad_ffn_shift = norm_pull(grad_inner_two)
    gelu_pull = jax.vjp(gelu_exact, hidden)[1]
    grad_hidden = gelu_pull(grad_activated)[0]
    hidden_low = grad_hidden.astype(jnp.bfloat16)
    grad_in_w = outer_sum(normed_two_low, hidden_low)
    grad_in_bias = jnp.sum(hidden_low.astype(jnp.float32), axis=0)
    grad_normed_two = times_transposed(hidden_low, in_w)
    second_pull = jax.vjp(layer_norm, middle, gains[2], shift_rows[5])[1]
    grad_middle_part, grad_gain_two, grad_shift_five = second_pull(grad_normed_two)
    grad_middle = upstream + grad_middle_part
    branch_low = grad_middle.astype(jnp.bfloat16)
    grad_out_w = outer_sum(inner_low, branch_low)
    grad_out_bias = jnp.sum(branch_low.astype(jnp.float32), axis=0)
    grad_inner = times_transposed(branch_low, out_w)
    inner_pull = jax.vjp(layer_norm, context, gains[1], shift_rows[3])[1]
    grad_context, grad_gain_one, grad_shift_three = inner_pull(grad_inner)
    context_grad_low = grad_context.astype(jnp.bfloat16).reshape(tok_rows, H, DH)
    delta = jnp.einsum("qhd,hqd->hq", context_grad_low.astype(jnp.float32), context3)

    def grad_pair(
        q_rows, grad_rows, lse_rows, delta_rows, qp, qs, key3, value3, k_places, k_segment
    ):
        scores = (
            jnp.einsum("qhd,khd->hqk", q_rows, key3, preferred_element_type=jnp.float32) * scaling
        )
        allowed = allowed_pairs(qp, qs, k_places, k_segment)
        probabilities = jnp.where(allowed, jnp.exp(scores - lse_rows[..., None]), 0.0)
        upstream_probs = jnp.einsum(
            "qhd,khd->hqk", grad_rows, value3, preferred_element_type=jnp.float32
        )
        score_grad = (probabilities * (upstream_probs - delta_rows[..., None])).astype(jnp.bfloat16)
        query_add = (
            jnp.einsum("hqk,khd->qhd", score_grad, key3, preferred_element_type=jnp.float32)
            * scaling
        )
        key_add = (
            jnp.einsum("hqk,qhd->khd", score_grad, q_rows, preferred_element_type=jnp.float32)
            * scaling
        )
        value_add = jnp.einsum(
            "hqk,qhd->khd",
            probabilities.astype(jnp.bfloat16),
            grad_rows,
            preferred_element_type=jnp.float32,
        )
        return (query_add, key_add, value_add)

    def grad_block(key3, value3, k_places, k_segment):
        return grad_pair(
            query3,
            context_grad_low,
            log_total,
            delta,
            q_places,
            q_segment,
            key3,
            value3,
            k_places,
            k_segment,
        )

    zero_query = jnp.zeros((tok_rows, H, DH), jnp.float32)
    gathered_keys, gathered_values = (
        lax.all_gather(keyed, "ctx", axis=0, tiled=True),
        lax.all_gather(valued, "ctx", axis=0, tiled=True),
    )
    stream_rows = gathered_keys.shape[0]
    block_rows = math.gcd(stream_rows, 512)
    block_count = stream_rows // block_rows
    all_places, all_segment = row_places(0, stream_rows, deal_row, bounds, group_rows)

    def sweep(query_grad, pieces):
        key3, value3, block_places, block_segment = pieces
        query_add, key_add, value_add = grad_block(key3, value3, block_places, block_segment)
        return (query_grad + query_add, (key_add, value_add))

    query_grad, (key_parts, value_parts) = lax.scan(
        sweep,
        zero_query,
        (
            gathered_keys.reshape(block_count, block_rows, H, DH),
            gathered_values.reshape(block_count, block_rows, H, DH),
            all_places.reshape(block_count, block_rows),
            all_segment.reshape(block_count, block_rows),
        ),
    )
    key_terms = key_parts.reshape(stream_rows, D)
    value_terms = value_parts.reshape(stream_rows, D)
    key_grad_mine, value_grad_mine = (
        lax.psum_scatter(
            key_terms.astype(jnp.bfloat16), "ctx", scatter_dimension=0, tiled=True
        ).astype(jnp.float32),
        lax.psum_scatter(
            value_terms.astype(jnp.bfloat16), "ctx", scatter_dimension=0, tiled=True
        ).astype(jnp.float32),
    )
    qkv_grad_low = jnp.concatenate(
        [query_grad.reshape(tok_rows, D), key_grad_mine, value_grad_mine], axis=1
    ).astype(jnp.bfloat16)
    grad_qkv_w = outer_sum(normed_low, qkv_grad_low)
    column_sums = jnp.sum(qkv_grad_low.astype(jnp.float32), axis=0)
    grad_query_bias = column_sums[:D]
    grad_value_bias = column_sums[2 * D :]
    grad_normed = times_transposed(qkv_grad_low, qkv_w)
    first_pull = jax.vjp(layer_norm, inputs, gains[0], shift_rows[0])[1]
    grad_inputs_part, grad_gain_zero, grad_shift_zero = first_pull(grad_normed)
    input_grad = grad_middle + grad_inputs_part
    gains_terms = jnp.stack([grad_gain_zero, grad_gain_one, grad_gain_two])
    shift_terms = jnp.stack(
        [
            grad_shift_zero,
            grad_query_bias,
            grad_value_bias,
            grad_shift_three,
            grad_out_bias,
            grad_shift_five,
            grad_back_bias,
        ]
    )
    ffn_shift_terms = jnp.stack([grad_in_bias, grad_ffn_shift])
    reduced = (
        lax.psum_scatter(grad_qkv_w, ("ctx", "fsdp"), scatter_dimension=0, tiled=True),
        lax.psum_scatter(grad_out_w, ("ctx", "fsdp"), scatter_dimension=0, tiled=True),
        lax.psum_scatter(grad_in_w, ("ctx", "fsdp"), scatter_dimension=0, tiled=True),
        lax.psum_scatter(grad_back_w, ("ctx", "fsdp"), scatter_dimension=0, tiled=True),
        lax.psum_scatter(gains_terms, ("ctx", "fsdp"), scatter_dimension=1, tiled=True),
        lax.psum_scatter(shift_terms, ("ctx", "fsdp"), scatter_dimension=1, tiled=True),
        lax.psum_scatter(grad_ffn_gain, ("ctx", "fsdp"), scatter_dimension=0, tiled=True),
        lax.psum_scatter(ffn_shift_terms, ("ctx", "fsdp"), scatter_dimension=1, tiled=True),
    )
    return (mixed_out[None], input_grad[None]) + tuple(reduced)


def solution(mesh):
    in_specs = (
        P("fsdp", "ctx", None),
        P("fsdp", "ctx", None),
        P("fsdp", None),
        P("fsdp", None),
        P("fsdp", None),
        P("fsdp", None),
        P("fsdp", None),
        P("fsdp", None),
        P(None, "fsdp"),
        P(None, "fsdp"),
        P("fsdp"),
        P(None, "fsdp"),
    )
    out_specs = (
        P("fsdp", "ctx", None),
        P("fsdp", "ctx", None),
        P(("ctx", "fsdp"), None),
        P(("ctx", "fsdp"), None),
        P(("ctx", "fsdp"), None),
        P(("ctx", "fsdp"), None),
        P(None, ("ctx", "fsdp")),
        P(None, ("ctx", "fsdp")),
        P(("ctx", "fsdp")),
        P(None, ("ctx", "fsdp")),
    )
    return jax.shard_map(local, mesh=mesh, in_specs=in_specs, out_specs=out_specs, check_vma=False)
```

profile of v0, /device:TPU:0, one launch (start us, length us, event | category | flops | bytes accessed | tf_op | source)
XLA Modules:
  0.0 1461.5 jit_solution(8794208688010352200)
XLA Ops:
  8.0 14.9 %all-gather.1 = bf16[4,192,7]{1,2,0:T(8,128)(2,1)S(1)} all-gather(bf16[1,192,7]{1,2,0:T(8,128)(2,1)} %bitcast.267), channel_id=1, replica_groups=mesh['ctx'=8,'fsdp'=4] {'fsdp'}, dimensions={0}, use_global_device_ids=true | all-gather | bytes 13440 | tf_op jit(solution)/shard_map/all_gather | solution.py:87
  23.0 12.2 all-gather
  38.9 43.6 %all-gather.10.cloned.1.call-done = bf16[768,2304]{1,0:T(8,128)(2,1)} async-done(((bf16[192,2304]{1,0:T(8,128)(2,1)}), bf16[768,2304]{1,0:T(8,128)(2,1)}) %all-gather.10.cloned.1.call-update) | async-done | bytes 3538960 | tf_op jit(solution)/shard_map/all_gather | solution.py:82
  95.8 13.0 all_gather.45
  109.5 13.6 all-gather.2
  124.2 10.1 all-gather.12.cloned.1.call-done
  134.3 8.6 copy.91
  142.9 7.5 copy.120
  155.3 26.5 %all-gather.14.cloned.1.call-done = bf16[4096,768]{1,0:T(8,128)(2,1)} async-done(((bf16[512,768]{1,0:T(8,128)(2,1)}), bf16[4096,768]{1,0:T(8,128)(2,1)}) %all-gather.14.cloned.1.call-update) | async-done | bytes 6291472 | tf_op jit(solution)/shard_map/all_gather | solution.py:111
  181.8 8.9 copy.93
  190.7 7.1 copy.121
  202.6 179.3 %while.30 = (s32[]{:T(128)}, f32[12,512]{1,0:T(8,128)S(1)}, f32[12,512]{1,0:T(8,128)S(1)}, f32[12,512,64]{1,2,0:T(8,128)}, s32[8,512]{1,0:T(8,128)S(1)}, /*index...) while((s32[]{:T(128)}, f32[12,512]{1,0:T(8,128)S(1)}, ...), condition=%wide.region_10.11_spmd.clone, body=%wide.region_7.10_spmd.clone.sunk | while | flops 848197632 | bytes 95043760 | solution.py:140
  202.9 8.0 fusion.150
  210.9 7.7 fusion.151
  225.0 8.0 fusion.150
  233.0 7.7 fusion.151
  247.4 8.0 fusion.150
  255.5 7.7 fusion.151
  269.9 8.0 fusion.150
  277.9 7.6 fusion.151
  292.3 8.0 fusion.150
  300.3 7.7 fusion.151
  314.7 8.0 fusion.150
  322.7 7.7 fusion.151
  337.1 8.0 fusion.150
  345.2 7.7 fusion.151
  359.6 8.0 fusion.150
  367.6 7.6 fusion.151
  389.9 21.5 %fusion.101 = (f32[512]{0:T(512)S(1)}, f32[512,3072]{1,0:T(8,128)}, f32[512,3072]{1,0:T(8,128)}, f32[512,3072]{1,0:T(8,128)}) fusion(f32[3072]{0:T(1024)S(1)} %bitcast.261, bf16[768,3072]{1,0:T(8,128)(2,1)} %all-gather.18.cloned.1.call-done, f32[512,768]{1,0:T(8,128)} %copy-done.10, f32[768]{0:T(1024)S(1)} %get-tuple-element.371, ...), kind=kOutput, calls=%fused_computation.205 | convolution fusion | flops 2521693696 | bytes 25190400 | tf_op jit(solution)/shard_map/dot_general | solution.py:150
  411.4 7.4 multiply_reduce_fusion.1
  422.2 10.8 convert_reduce_fusion
  434.6 6.0 multiply_reduce_fusion.3
  447.7 251.0 %while.31 = (s32[]{:T(128)}, f32[512,12,64]{0,2,1:T(8,128)}, bf16[8,512,12,64]{1,3,2,0:T(8,128)(2,1)}, bf16[8,512,12,64]{1,3,2,0:T(8,128)(2,1)}, bf16[8,512,12,6...) while((s32[]{:T(128)}, f32[512,12,64]{0,2,1:T(8,128)}, ...), condition=%wide.region_24.25_spmd.clone, body=%wide.region_23.24_spmd.clone.sunk | while | flops 2047082496 | bytes 195125520 | solution.py:249
  455.7 8.4 fusion.165
  486.7 8.4 fusion.165
  495.1 5.9 bitcast_add_fusion.2
  518.1 8.4 fusion.165
  526.5 5.9 bitcast_add_fusion.2
  549.4 8.4 fusion.165
  557.9 5.9 bitcast_add_fusion.2
  580.8 8.4 fusion.165
  589.3 5.9 bitcast_add_fusion.2
  612.1 8.4 fusion.165
  620.6 5.9 bitcast_add_fusion.2
  643.5 8.4 fusion.165
  652.0 5.9 bitcast_add_fusion.2
  674.9 8.4 fusion.165
  683.4 5.9 bitcast_add_fusion.2
  698.7 6.9 copy.101
  705.6 6.8 copy.123
  712.9 6.9 copy.100
  719.8 7.1 copy.122
  733.2 7.2 fusion.95
  742.3 6.2 fusion.66
  750.1 24.5 %reduce-scatter.14.cloned.1.call-done = bf16[512,768]{0,1:T(8,128)(2,1)} async-done(((bf16[4096,768]{0,1:T(8,128)(2,1)}), bf16[512,768]{0,1:T(8,128)(2,1)}) %reduce-scatter.14.cloned.1.call-update) | async-done | bytes 786448 | tf_op jit(solution)/shard_map/reduce_scatter | solution.py:265
  774.6 65.5 %reduce-scatter.12.cloned.1.call-done = bf16[512,768]{0,1:T(8,128)(2,1)} async-done(((bf16[4096,768]{0,1:T(8,128)(2,1)}), bf16[512,768]{0,1:T(8,128)(2,1)}) %reduce-scatter.12.cloned.1.call-update) | async-done | bytes 786448 | tf_op jit(solution)/shard_map/reduce_scatter | solution.py:262
  840.1 6.6 fusion.88
  848.2 6.8 fusion.64
  855.0 87.4 %reduce-scatter.24.cloned.1.call-done = f32[96,2]{1,0:T(8,128)} async-done(((f32[3072,2]{1,0:T(8,128)}), f32[96,2]{1,0:T(8,128)}) %reduce-scatter.24.cloned.1.call-update) | async-done | bytes 784
  952.3 40.7 %all-reduce.3 = (f32[3,768]{1,0:T(4,128)S(1)}, f32[7,768]{1,0:T(8,128)S(1)}, f32[3072]{0:T(1024)S(1)}) all-reduce(f32[3,768]{1,0:T(4,128)S(1)} %pad_maximum_fusion.2, f32[7,768]{1,0:T(8,128)S(1)} %stack.36, f32[3072]{0:T(1024)S(1)} %copy-done.25), channel_id=8, replica_groups=mesh['ctx'=8,'fsdp'=4] {'ctx','fsdp'}, use_global_device_ids=true, to_apply=%region_36.37.clone | all-reduce | flops 10752 | bytes 86016
  994.9 51.3 %reduce-scatter.18.cloned.1.call-done = f32[24,768]{1,0:T(8,128)} async-done(((f32[768,768]{1,0:T(8,128)}), f32[24,768]{1,0:T(8,128)}) %reduce-scatter.18.cloned.1.call-update) | async-done | bytes 73744 | tf_op jit(solution)/shard_map/reduce_scatter | solution.py:295
  1046.2 142.2 %reduce-scatter.20.cloned.1.call-done = f32[24,3072]{1,0:T(8,128)} async-done(((f32[768,3072]{1,0:T(8,128)}), f32[24,3072]{1,0:T(8,128)}) %reduce-scatter.20.cloned.1.call-update) | async-done | bytes 294928 | tf_op jit(solution)/shard_map/reduce_scatter | solution.py:296
  1188.4 140.8 %reduce-scatter.22.cloned.1.call-done = f32[96,768]{1,0:T(8,128)} async-done(((f32[3072,768]{1,0:T(8,128)}), f32[96,768]{1,0:T(8,128)}) %reduce-scatter.22.cloned.1.call-update) | async-done | bytes 294928 | tf_op jit(solution)/shard_map/reduce_scatter | solution.py:297
  1329.2 125.6 %reduce-scatter.16.cloned.1.call-done = f32[24,2304]{1,0:T(8,128)} async-done(((f32[768,2304]{1,0:T(8,128)}), f32[24,2304]{1,0:T(8,128)}) %reduce-scatter.16.cloned.1.call-update) | async-done | bytes 221200 | tf_op jit(solution)/shard_map/reduce_scatter | solution.py:294
  (371 shorter events, 267.5 us)
Async XLA Ops:
  7.2 75.3 %all-gather.10.cloned.1.call-start = ((), (), s32[]{:S(2)}) async-start(), calls=%async_computation.7 | async-start | bytes 4423680 | tf_op jit(solution)/shard_map/all_gather | solution.py:82
  7.9 126.4 %all-gather.12.cloned.1.call-start = ((), (), s32[]{:S(2)}) async-start(), calls=%async_computation.8 | async-start | bytes 7077888 | tf_op jit(solution)/shard_map/all_gather | solution.py:110
  35.4 51.5 %copy-start.26 = (f32[768]{0:T(1024)}, f32[768]{0:T(1024)S(1)}, u32[]{:S(2)}) copy-start(f32[768]{0:T(1024)S(1)} %get-tuple-element.379) | copy-start | bytes 9220
  36.0 50.9 %copy-start.39 = (f32[768]{0:T(1024)}, f32[768]{0:T(1024)S(1)}, u32[]{:S(2)}) copy-start(f32[768]{0:T(1024)S(1)} %get-tuple-element.376) | copy-start | bytes 9220
  36.0 349.6 %copy-start.43 = (f32[768]{0:T(1024)}, f32[768]{0:T(1024)S(1)}, u32[]{:S(2)}) copy-start(f32[768]{0:T(1024)S(1)} %get-tuple-element.373) | copy-start | bytes 9220
  36.0 353.9 %copy-start.41 = (f32[768]{0:T(1024)}, f32[768]{0:T(1024)S(1)}, u32[]{:S(2)}) copy-start(f32[768]{0:T(1024)S(1)} %get-tuple-element.371) | copy-start | bytes 9220
  37.3 49.5 %copy-start.28 = (f32[512]{0:T(512)}, f32[512]{0:T(512)S(1)}, u32[]{:S(2)}) copy-start(f32[512]{0:T(512)S(1)} %broadcast_multiply_fusion.4) | copy-start | bytes 6148
  38.8 48.0 %copy-start.32 = (f32[512]{0:T(512)}, f32[512]{0:T(512)S(1)}, u32[]{:S(2)}) copy-start(f32[512]{0:T(512)S(1)} %fusion.57) | copy-start | bytes 6148
  38.8 48.0 %copy-start.30 = (f32[512]{0:T(512)}, f32[512]{0:T(512)S(1)}, u32[]{:S(2)}) copy-start(f32[512]{0:T(512)S(1)} %fusion.83) | copy-start | bytes 6148
  90.1 5.0 copy-start.50
  90.1 5.2 copy-start.53
  90.1 5.7 copy-start.49
  90.1 19.4 %copy-start.51 = (bf16[768]{0:T(1024)(128)(2,1)S(1)}, bf16[768]{0:T(1024)(128)(2,1)}, u32[]{:S(2)}) copy-start(bf16[768]{0:T(1024)(128)(2,1)} %param.26) | copy-start | bytes 4612
  90.1 91.7 %all-gather.14.cloned.1.call-start = ((), (), s32[]{:S(2)}) async-start(), calls=%async_computation.9 | async-start | bytes 7077888 | tf_op jit(solution)/shard_map/all_gather | solution.py:111
  93.2 292.3 %all-gather.16.cloned.1.call-start = ((), (), s32[]{:S(2)}) async-start(), calls=%async_computation.10 | async-start | bytes 1474560 | tf_op jit(solution)/shard_map/all_gather | solution.py:83
  93.8 296.1 %all-gather.18.cloned.1.call-start = ((), (), s32[]{:S(2)}) async-start(), calls=%async_computation.11 | async-start | bytes 5898240 | tf_op jit(solution)/shard_map/all_gather | solution.py:84
  94.4 317.0 %all-gather.20.cloned.1.call-start = ((), (), s32[]{:S(2)}) async-start(), calls=%async_computation.12 | async-start | bytes 5898240 | tf_op jit(solution)/shard_map/all_gather | solution.py:85
  94.9 679.7 %reduce-scatter.14.cloned.1.call-start = ((), (), s32[]{:S(2)}) async-start(), calls=%async_computation.14 | async-start | bytes 7077888 | tf_op jit(solution)/shard_map/reduce_scatter | solution.py:265
  210.9 8.3 copy-start
  233.0 8.4 copy-start
  255.5 8.4 copy-start
  277.9 8.3 copy-start
  300.3 8.3 copy-start
  322.7 8.4 copy-start
  345.1 8.4 copy-start
  367.6 8.3 copy-start
  389.9 21.5 %copy-start.19 = (bf16[1,512,768]{2,1,0:T(8,128)(2,1)S(1)}, bf16[1,512,768]{2,1,0:T(8,128)(2,1)}, u32[]{:S(2)}) copy-start(bf16[1,512,768]{2,1,0:T(8,128)(2,1)} %param.17) | copy-start | bytes 2359300
  411.4 7.4 copy-start.5
  422.2 12.4 copy-start.11
  451.1 4.6 copy-start.2
  464.1 5.4 copy-start.1
  464.1 10.3 copy-start.3
  482.1 4.6 copy-start.2
  495.1 5.9 copy-start.1
  495.1 10.6 copy-start.3
  513.5 4.6 copy-start.2
  526.5 5.9 copy-start.1
  526.5 10.6 copy-start.3
  544.8 4.6 copy-start.2
  557.9 5.9 copy-start.1
  557.9 10.6 copy-start.3
  576.2 4.6 copy-start.2
  589.3 5.9 copy-start.1
  589.3 10.6 copy-start.3
  620.6 5.9 copy-start.1
  620.6 10.7 copy-start.3
  652.0 5.9 copy-start.1
  652.0 10.7 copy-start.3
  683.4 5.9 copy-start.1
  683.4 10.6 copy-start.3
  712.4 127.7 %reduce-scatter.12.cloned.1.call-start = ((), (), s32[]{:S(2)}) async-start(), calls=%async_computation.13 | async-start | bytes 7077888 | tf_op jit(solution)/shard_map/reduce_scatter | solution.py:262
  727.0 215.4 %reduce-scatter.24.cloned.1.call-start = ((), (), s32[]{:S(2)}) async-start(), calls=%async_computation.19 | async-start | bytes 1622016
  729.4 316.8 %reduce-scatter.18.cloned.1.call-start = ((), (), s32[]{:S(2)}) async-start(), calls=%async_computation.16 | async-start | bytes 2433024 | tf_op jit(solution)/shard_map/reduce_scatter | solution.py:295
  733.2 455.3 %reduce-scatter.20.cloned.1.call-start = ((), (), s32[]{:S(2)}) async-start(), calls=%async_computation.17 | async-start | bytes 9732096 | tf_op jit(solution)/shard_map/reduce_scatter | solution.py:296
  740.5 588.7 %reduce-scatter.22.cloned.1.call-start = ((), (), s32[]{:S(2)}) async-start(), calls=%async_computation.18 | async-start | bytes 9732096 | tf_op jit(solution)/shard_map/reduce_scatter | solution.py:297
  748.6 91.6 %copy-start.9 = (bf16[1,512,768]{2,1,0:T(8,128)(2,1)S(1)}, bf16[1,512,768]{2,1,0:T(8,128)(2,1)}, u32[]{:S(2)}) copy-start(bf16[1,512,768]{2,1,0:T(8,128)(2,1)} %param.16) | copy-start | bytes 2359300
  748.6 91.6 %copy-start.27 = (f32[768]{0:T(1024)S(1)}, f32[768]{0:T(1024)}, u32[]{:S(2)}) copy-start(f32[768]{0:T(1024)} %copy-done.26) | copy-start | bytes 9220
  748.6 91.6 %copy-start.29 = (f32[512]{0:T(512)S(1)}, f32[512]{0:T(512)}, u32[]{:S(2)}) copy-start(f32[512]{0:T(512)} %copy-done.28) | copy-start | bytes 6148
  748.6 91.6 %copy-start.31 = (f32[512]{0:T(512)S(1)}, f32[512]{0:T(512)}, u32[]{:S(2)}) copy-start(f32[512]{0:T(512)} %copy-done.30) | copy-start | bytes 6148
  748.6 91.6 %copy-start.40 = (f32[768]{0:T(1024)S(1)}, f32[768]{0:T(1024)}, u32[]{:S(2)}) copy-start(f32[768]{0:T(1024)} %copy-done.39) | copy-start | bytes 9220
  748.6 706.2 %reduce-scatter.16.cloned.1.call-start = ((), (), s32[]{:S(2)}) async-start(), calls=%async_computation.15 | async-start | bytes 7299072 | tf_op jit(solution)/shard_map/reduce_scatter | solution.py:294
  943.8 4.9 copy-start.33
  943.8 5.8 copy-start.21
  943.8 5.8 copy-start.23
  (31 other events, 69.5 us)
Sparse Core Ops, SparseCore 0:
  9.6 72.8 all-gather.9
  90.2 44.0 all-gather.11
  136.2 45.5 all-gather.13
  183.2 30.4 all-gather.15
  215.1 88.5 all-gather.17
  305.1 87.8 all-gather.19
  712.5 62.0 reduce-scatter.13
  778.4 61.7 reduce-scatter.11
  845.4 96.9 reduce-scatter.23
  948.1 98.0 reduce-scatter.17
  1053.7 134.6 reduce-scatter.19
  1194.8 134.4 reduce-scatter.21
  1336.4 118.3 reduce-scatter.15
where the time goes:
time: 1470 us; the launch traced here: 1460 us
  waiting for transfers between devices  720 us (49%)
  matrix products  403 us (27%)
  local copies, waits for them, and re-layouts  131 us (9%)
  other arithmetic  96.1 us (7%)
  blocking collectives  94.5 us (6%)
  between operations  14.9 us (1%)
    reduce_scatter x1, waiting for transfers between devices, local(): lax.psum_scatter(grad_in_w, ('ctx', 'fsdp'), scatter_dimension=0, tiled=T...  142 us
    reduce_scatter x1, waiting for transfers between devices, local(): lax.psum_scatter(grad_back_w, ('ctx', 'fsdp'), scatter_dimension=0, tiled...  141 us
    reduce_scatter x1, waiting for transfers between devices, local(): lax.psum_scatter(grad_qkv_w, ('ctx', 'fsdp'), scatter_dimension=0, tiled=...  126 us
    unnamed x14, waiting for transfers between devices  89.8 us
    dot_general x8, matrix products, grad_pair(): jnp.einsum('qhd,khd->hqk', grad_rows, value3, preferred_element_type=jnp....  67.5 us
    reduce_scatter x1, waiting for transfers between devices, local(): lax.psum_scatter(key_terms.astype(jnp.bfloat16), 'ctx', scatter_dimension...  65.5 us
    dot_general x8, matrix products, visit_block(): jnp.einsum('qhd,khd->hqk', query3, key3, preferred_element_type=jnp.float32)  64 us
    reduce_sum x8, other arithmetic, visit_block(): totals = totals * rescale + jnp.sum(expo, axis=-1)  61.3 us
  transfers between devices with their start and end apart: 13, of which 10 were waited for; matrix products, arithmetic and copies ran while one was open for 21% of the time, Pallas kernels for 0%

commit v1 on v0

--- a/solution.py
+++ b/solution.py
@@ -107,8 +107,11 @@
         jnp.zeros((H, tok_rows), jnp.float32),
         jnp.zeros((H, tok_rows, DH), jnp.float32),
     )
-    key_rows = lax.all_gather(keyed, "ctx", axis=0, tiled=True)
-    value_rows = lax.all_gather(valued, "ctx", axis=0, tiled=True)
+    key_rows, value_rows = jnp.split(
+        lax.all_gather(jnp.concatenate([keyed, valued], axis=1), "ctx", axis=0, tiled=True),
+        [keyed.shape[1]],
+        axis=1,
+    )
     key_count = key_rows.shape[0]
     block_rows = 512
     block_count = key_count // block_rows

time: 1470 us -> 1570 us (1.068)
  local copies, waits for them, and re-layouts: 131 us -> 185 us
  waiting for transfers between devices: 720 us -> 770 us
    all_gather x2 -> x3, waiting for transfers between devices: 36.6 us -> 86.3 us  [the longest x1 52.2 us: local(): lax.all_gather(jnp.concatenate([keyed, valued], axis=1), 'ctx', axis=0, t...]
    split x0 -> x3, local copies, waits for them, and re-layouts: none -> 28.2 us  [local(): jnp.split(lax.all_gather(jnp.concatenate([keyed, valued], axis=1), 'ctx',...]
    unnamed x112 -> x120, local copies, waits for them, and re-layouts: 54 us -> 78.9 us
    unnamed x14 -> x15, waiting for transfers between devices: 89.8 us -> 89.9 us
  transfers between devices with their start and end apart: 13 -> 14, of which waited for: 10 -> 11; matrix products, arithmetic and copies ran while one was open for 21% -> 23% of each run, Pallas kernels for 0% -> 0%
where the time goes in v1:
time: 1570 us
  waiting for transfers between devices  770 us (49%)
  matrix products  403 us (26%)
  local copies, waits for them, and re-layouts  185 us (12%)
  other arithmetic  99.1 us (6%)
  blocking collectives  94.2 us (6%)
    reduce_scatter x1, waiting for transfers between devices, local(): lax.psum_scatter(grad_in_w, ('ctx', 'fsdp'), scatter_dimension=0, tiled=T...  142 us
    reduce_scatter x1, waiting for transfers between devices, local(): lax.psum_scatter(grad_back_w, ('ctx', 'fsdp'), scatter_dimension=0, tiled...  141 us
    reduce_scatter x1, waiting for transfers between devices, local(): lax.psum_scatter(grad_qkv_w, ('ctx', 'fsdp'), scatter_dimension=0, tiled=...  125 us
    unnamed x15, waiting for transfers between devices  89.9 us
    unnamed x120, local copies, waits for them, and re-layouts  78.9 us
    dot_general x8, matrix products, grad_pair(): jnp.einsum('qhd,khd->hqk', grad_rows, value3, preferred_element_type=jnp....  67.5 us
    reduce_scatter x1, waiting for transfers between devices, local(): lax.psum_scatter(key_terms.astype(jnp.bfloat16), 'ctx', scatter_dimension...  65.6 us
    dot_general x8, matrix products, visit_block(): jnp.einsum('qhd,khd->hqk', query3, key3, preferred_element_type=jnp.float32)  64 us
  transfers between devices with their start and end apart: 14, of which 11 were waited for; matrix products, arithmetic and copies ran while one was open for 23% of the time, Pallas kernels for 0%

profile of v1, /device:TPU:0, one launch (start us, length us, event | category | flops | bytes accessed | tf_op | source)
XLA Modules:
  0.0 1568.3 jit_solution(6162188369739779520)
XLA Ops:
  8.0 14.9 all-gather.1
  23.0 12.2 all-gather
  38.9 43.6 %all-gather.11.cloned.1.call-done = bf16[768,2304]{1,0:T(8,128)(2,1)} async-done(((bf16[192,2304]{1,0:T(8,128)(2,1)}), bf16[768,2304]{1,0:T(8,128)(2,1)}) %all-gather.11.cloned.1.call-update) | async-done | bytes 3538960 | tf_op jit(solution)/shard_map/all_gather | solution.py:82
  98.4 13.0 all_gather.45
  112.1 13.3 all-gather.2
  127.2 7.0 all-gather.21.cloned.1.call-done
  134.2 8.6 copy.103
  142.8 7.5 copy.130
  155.2 27.0 %all-gather.23.cloned.1.call-done = bf16[4096,768]{1,0:T(8,128)(2,1)} async-done(((bf16[512,768]{1,0:T(8,128)(2,1)}), bf16[4096,768]{1,0:T(8,128)(2,1)}) %all-gather.23.cloned.1.call-update) | async-done | bytes 6291472 | tf_op jit(solution)/shard_map/all_gather | solution.py:240
  182.3 9.1 copy.104
  191.4 7.7 copy.131
  204.0 52.2 %all-gather.13.cloned.1.call-done = bf16[4096,1536]{1,0:T(8,128)(2,1)} async-done(((bf16[512,1536]{1,0:T(8,128)(2,1)}), bf16[4096,1536]{1,0:T(8,128)(2,1)}) %all-gather.13.cloned.1.call-update) | async-done | bytes 12582928 | tf_op jit(solution)/shard_map/all_gather | solution.py:111
  256.2 10.4 fusion.104
  266.5 8.9 copy.97
  275.5 7.0 copy.128
  287.3 8.9 copy.99
  296.2 7.4 copy.129
  308.6 180.4 %while.30 = (s32[]{:T(128)}, f32[12,512]{1,0:T(8,128)S(1)}, f32[12,512]{1,0:T(8,128)S(1)}, f32[12,512,64]{1,2,0:T(8,128)}, s32[8,512]{1,0:T(8,128)S(1)}, /*index...) while((s32[]{:T(128)}, f32[12,512]{1,0:T(8,128)S(1)}, ...), condition=%wide.region_10.11_spmd.clone, body=%wide.region_7.10_spmd.clone.sunk | while | flops 848197632 | bytes 95043760 | solution.py:143
  308.9 8.0 fusion.151
  316.9 7.7 fusion.152
  331.1 8.0 fusion.151
  339.1 7.7 fusion.152
  353.6 8.0 fusion.151
  361.6 7.7 fusion.152
  375.9 8.0 fusion.151
  383.9 7.8 fusion.152
  399.3 8.0 fusion.151
  407.3 7.7 fusion.152
  421.7 8.0 fusion.151
  429.8 7.6 fusion.152
  444.2 8.0 fusion.151
  452.2 7.7 fusion.152
  466.5 8.0 fusion.151
  474.6 7.7 fusion.152
  497.0 21.5 %fusion.101 = (f32[512]{0:T(512)S(1)}, f32[512,3072]{1,0:T(8,128)}, f32[512,3072]{1,0:T(8,128)}, f32[512,3072]{1,0:T(8,128)}) fusion(f32[3072]{0:T(1024)S(1)} %bitcast.275, bf16[768,3072]{1,0:T(8,128)(2,1)} %all-gather.17.cloned.1.call-done, f32[512,768]{1,0:T(8,128)} %copy-done.11, f32[768]{0:T(1024)S(1)} %get-tuple-element.371, ...), kind=kOutput, calls=%fused_computation.206 | convolution fusion | flops 2521693696 | bytes 25190400 | tf_op jit(solution)/shard_map/dot_general | solution.py:153
  518.5 7.4 multiply_reduce_fusion.1
  529.3 10.6 convert_reduce_fusion
  541.5 6.0 multiply_reduce_fusion.3
  554.7 251.2 %while.31 = (s32[]{:T(128)}, f32[512,12,64]{0,2,1:T(8,128)}, bf16[8,512,12,64]{1,3,2,0:T(8,128)(2,1)}, bf16[8,512,12,64]{1,3,2,0:T(8,128)(2,1)}, bf16[8,512,12,6...) while((s32[]{:T(128)}, f32[512,12,64]{0,2,1:T(8,128)}, ...), condition=%wide.region_24.25_spmd.clone, body=%wide.region_23.24_spmd.clone.sunk | while | flops 2047082496 | bytes 195125520 | solution.py:252
  562.7 8.4 fusion.166
  593.7 8.4 fusion.166
  625.1 8.4 fusion.166
  656.4 8.4 fusion.166
  664.9 5.9 bitcast_add_fusion.2
  687.8 8.4 fusion.166
  719.1 8.4 fusion.166
  750.5 8.4 fusion.166
  781.9 8.4 fusion.166
  805.9 6.9 copy.109
  812.8 6.8 copy.133
  819.8 6.9 copy.108
  826.8 7.2 copy.132
  840.2 7.2 fusion.95
  849.3 6.2 fusion.66
  857.2 24.6 %reduce-scatter.14.cloned.1.call-done = bf16[512,768]{0,1:T(8,128)(2,1)} async-done(((bf16[4096,768]{0,1:T(8,128)(2,1)}), bf16[512,768]{0,1:T(8,128)(2,1)}) %reduce-scatter.14.cloned.1.call-update) | async-done | bytes 786448 | tf_op jit(solution)/shard_map/reduce_scatter | solution.py:268
  881.7 65.6 %reduce-scatter.12.cloned.1.call-done = bf16[512,768]{0,1:T(8,128)(2,1)} async-done(((bf16[4096,768]{0,1:T(8,128)(2,1)}), bf16[512,768]{0,1:T(8,128)(2,1)}) %reduce-scatter.12.cloned.1.call-update) | async-done | bytes 786448 | tf_op jit(solution)/shard_map/reduce_scatter | solution.py:265
  947.3 6.6 fusion.88
  955.3 6.8 fusion.64
  962.1 87.3 %reduce-scatter.24.cloned.1.call-done = f32[96,2]{1,0:T(8,128)} async-done(((f32[3072,2]{1,0:T(8,128)}), f32[96,2]{1,0:T(8,128)}) %reduce-scatter.24.cloned.1.call-update) | async-done | bytes 784
  1059.3 40.7 %all-reduce.3 = (f32[3,768]{1,0:T(4,128)S(1)}, f32[7,768]{1,0:T(8,128)S(1)}, f32[3072]{0:T(1024)S(1)}) all-reduce(f32[3,768]{1,0:T(4,128)S(1)} %pad_maximum_fusion.3, f32[7,768]{1,0:T(8,128)S(1)} %stack.36, f32[3072]{0:T(1024)S(1)} %copy-done.27), channel_id=8, replica_groups=mesh['ctx'=8,'fsdp'=4] {'ctx','fsdp'}, use_global_device_ids=true, to_apply=%region_36.37.clone | all-reduce | flops 10752 | bytes 86016
  1101.9 51.4 %reduce-scatter.18.cloned.1.call-done = f32[24,768]{1,0:T(8,128)} async-done(((f32[768,768]{1,0:T(8,128)}), f32[24,768]{1,0:T(8,128)}) %reduce-scatter.18.cloned.1.call-update) | async-done | bytes 73744 | tf_op jit(solution)/shard_map/reduce_scatter | solution.py:298
  1153.3 141.9 %reduce-scatter.20.cloned.1.call-done = f32[24,3072]{1,0:T(8,128)} async-done(((f32[768,3072]{1,0:T(8,128)}), f32[24,3072]{1,0:T(8,128)}) %reduce-scatter.20.cloned.1.call-update) | async-done | bytes 294928 | tf_op jit(solution)/shard_map/reduce_scatter | solution.py:299
  1295.2 141.1 %reduce-scatter.22.cloned.1.call-done = f32[96,768]{1,0:T(8,128)} async-done(((f32[3072,768]{1,0:T(8,128)}), f32[96,768]{1,0:T(8,128)}) %reduce-scatter.22.cloned.1.call-update) | async-done | bytes 294928 | tf_op jit(solution)/shard_map/reduce_scatter | solution.py:300
  1436.3 125.3 %reduce-scatter.16.cloned.1.call-done = f32[24,2304]{1,0:T(8,128)} async-done(((f32[768,2304]{1,0:T(8,128)}), f32[24,2304]{1,0:T(8,128)}) %reduce-scatter.16.cloned.1.call-update) | async-done | bytes 221200 | tf_op jit(solution)/shard_map/reduce_scatter | solution.py:297
  (386 shorter events, 316.1 us)
Async XLA Ops:
  7.2 75.3 %all-gather.11.cloned.1.call-start = ((), (), s32[]{:S(2)}) async-start(), calls=%async_computation.7 | async-start | bytes 4423680 | tf_op jit(solution)/shard_map/all_gather | solution.py:82
  7.9 126.3 %all-gather.21.cloned.1.call-start = ((), (), s32[]{:S(2)}) async-start(), calls=%async_computation.12 | async-start | bytes 7077888 | tf_op jit(solution)/shard_map/all_gather | solution.py:239
  35.4 51.5 %copy-start.28 = (f32[768]{0:T(1024)}, f32[768]{0:T(1024)S(1)}, u32[]{:S(2)}) copy-start(f32[768]{0:T(1024)S(1)} %get-tuple-element.379) | copy-start | bytes 9220
  36.0 50.9 %copy-start.41 = (f32[768]{0:T(1024)}, f32[768]{0:T(1024)S(1)}, u32[]{:S(2)}) copy-start(f32[768]{0:T(1024)S(1)} %get-tuple-element.376) | copy-start | bytes 9220
  36.0 456.7 %copy-start.45 = (f32[768]{0:T(1024)}, f32[768]{0:T(1024)S(1)}, u32[]{:S(2)}) copy-start(f32[768]{0:T(1024)S(1)} %get-tuple-element.373) | copy-start | bytes 9220
  36.0 461.0 %copy-start.43 = (f32[768]{0:T(1024)}, f32[768]{0:T(1024)S(1)}, u32[]{:S(2)}) copy-start(f32[768]{0:T(1024)S(1)} %get-tuple-element.371) | copy-start | bytes 9220
  37.3 49.5 %copy-start.30 = (f32[512]{0:T(512)}, f32[512]{0:T(512)S(1)}, u32[]{:S(2)}) copy-start(f32[512]{0:T(512)S(1)} %broadcast_multiply_fusion.4) | copy-start | bytes 6148
  38.8 48.0 %copy-start.34 = (f32[512]{0:T(512)}, f32[512]{0:T(512)S(1)}, u32[]{:S(2)}) copy-start(f32[512]{0:T(512)S(1)} %fusion.57) | copy-start | bytes 6148
  38.8 48.0 %copy-start.32 = (f32[512]{0:T(512)}, f32[512]{0:T(512)S(1)}, u32[]{:S(2)}) copy-start(f32[512]{0:T(512)S(1)} %fusion.83) | copy-start | bytes 6148
  90.0 92.2 %all-gather.23.cloned.1.call-start = ((), (), s32[]{:S(2)}) async-start(), calls=%async_computation.13 | async-start | bytes 7077888 | tf_op jit(solution)/shard_map/all_gather | solution.py:240
  93.1 4.6 copy-start.52
  93.1 4.7 copy-start.55
  93.1 5.3 copy-start.51
  93.1 19.0 %copy-start.53 = (bf16[768]{0:T(1024)(128)(2,1)S(1)}, bf16[768]{0:T(1024)(128)(2,1)}, u32[]{:S(2)}) copy-start(bf16[768]{0:T(1024)(128)(2,1)} %param.26) | copy-start | bytes 4612
  93.2 163.0 %all-gather.13.cloned.1.call-start = ((), (), s32[]{:S(2)}) async-start(), calls=%async_computation.8 | async-start | bytes 14155776 | tf_op jit(solution)/shard_map/all_gather | solution.py:111
  95.7 397.0 %all-gather.15.cloned.1.call-start = ((), (), s32[]{:S(2)}) async-start(), calls=%async_computation.9 | async-start | bytes 1474560 | tf_op jit(solution)/shard_map/all_gather | solution.py:83
  96.3 400.7 %all-gather.17.cloned.1.call-start = ((), (), s32[]{:S(2)}) async-start(), calls=%async_computation.10 | async-start | bytes 5898240 | tf_op jit(solution)/shard_map/all_gather | solution.py:84
  96.8 421.7 %all-gather.19.cloned.1.call-start = ((), (), s32[]{:S(2)}) async-start(), calls=%async_computation.11 | async-start | bytes 5898240 | tf_op jit(solution)/shard_map/all_gather | solution.py:85
  97.6 784.1 %reduce-scatter.14.cloned.1.call-start = ((), (), s32[]{:S(2)}) async-start(), calls=%async_computation.15 | async-start | bytes 7077888 | tf_op jit(solution)/shard_map/reduce_scatter | solution.py:268
  316.9 8.4 copy-start
  339.1 8.4 copy-start
  361.6 8.3 copy-start
  383.9 9.3 copy-start
  407.3 8.4 copy-start
  429.7 8.4 copy-start
  452.2 8.3 copy-start
  474.6 8.3 copy-start
  497.0 21.5 %copy-start.20 = (bf16[1,512,768]{2,1,0:T(8,128)(2,1)S(1)}, bf16[1,512,768]{2,1,0:T(8,128)(2,1)}, u32[]{:S(2)}) copy-start(bf16[1,512,768]{2,1,0:T(8,128)(2,1)} %param.17) | copy-start | bytes 2359300
  497.0 21.5 %copy-start.25 = (f32[4,1,768]{2,1,0:T(1,128)S(1)}, f32[4,1,768]{2,1,0:T(1,128)}, u32[]{:S(2)}) copy-start(f32[4,1,768]{2,1,0:T(1,128)} %convert_element_type.127) | copy-start | bytes 36868
  518.5 7.4 copy-start.5
  529.3 12.2 copy-start.12
  558.1 4.6 copy-start.2
  571.1 5.4 copy-start.1
  571.1 10.3 copy-start.3
  589.1 4.6 copy-start.2
  602.1 5.9 copy-start.1
  602.1 10.6 copy-start.3
  620.5 4.6 copy-start.2
  633.5 5.9 copy-start.1
  633.5 10.6 copy-start.3
  664.9 5.9 copy-start.1
  664.9 10.6 copy-start.3
  696.2 5.9 copy-start.1
  696.2 10.6 copy-start.3
  727.6 5.9 copy-start.1
  727.6 10.7 copy-start.3
  759.0 5.9 copy-start.1
  759.0 10.7 copy-start.3
  790.4 5.9 copy-start.1
  790.4 10.6 copy-start.3
  819.6 127.6 %reduce-scatter.12.cloned.1.call-start = ((), (), s32[]{:S(2)}) async-start(), calls=%async_computation.14 | async-start | bytes 7077888 | tf_op jit(solution)/shard_map/reduce_scatter | solution.py:265
  834.0 215.4 %reduce-scatter.24.cloned.1.call-start = ((), (), s32[]{:S(2)}) async-start(), calls=%async_computation.20 | async-start | bytes 1622016
  836.4 316.8 %reduce-scatter.18.cloned.1.call-start = ((), (), s32[]{:S(2)}) async-start(), calls=%async_computation.17 | async-start | bytes 2433024 | tf_op jit(solution)/shard_map/reduce_scatter | solution.py:298
  840.2 455.0 %reduce-scatter.20.cloned.1.call-start = ((), (), s32[]{:S(2)}) async-start(), calls=%async_computation.18 | async-start | bytes 9732096 | tf_op jit(solution)/shard_map/reduce_scatter | solution.py:299
  847.5 588.8 %reduce-scatter.22.cloned.1.call-start = ((), (), s32[]{:S(2)}) async-start(), calls=%async_computation.19 | async-start | bytes 9732096 | tf_op jit(solution)/shard_map/reduce_scatter | solution.py:300
  855.6 91.7 %copy-start.9 = (bf16[1,512,768]{2,1,0:T(8,128)(2,1)S(1)}, bf16[1,512,768]{2,1,0:T(8,128)(2,1)}, u32[]{:S(2)}) copy-start(bf16[1,512,768]{2,1,0:T(8,128)(2,1)} %param.16) | copy-start | bytes 2359300
  855.6 91.7 %copy-start.29 = (f32[768]{0:T(1024)S(1)}, f32[768]{0:T(1024)}, u32[]{:S(2)}) copy-start(f32[768]{0:T(1024)} %copy-done.28) | copy-start | bytes 9220
  855.6 91.7 %copy-start.31 = (f32[512]{0:T(512)S(1)}, f32[512]{0:T(512)}, u32[]{:S(2)}) copy-start(f32[512]{0:T(512)} %copy-done.30) | copy-start | bytes 6148
  855.6 91.7 %copy-start.33 = (f32[512]{0:T(512)S(1)}, f32[512]{0:T(512)}, u32[]{:S(2)}) copy-start(f32[512]{0:T(512)} %copy-done.32) | copy-start | bytes 6148
  855.6 91.7 %copy-start.42 = (f32[768]{0:T(1024)S(1)}, f32[768]{0:T(1024)}, u32[]{:S(2)}) copy-start(f32[768]{0:T(1024)} %copy-done.41) | copy-start | bytes 9220
  855.6 706.0 %reduce-scatter.16.cloned.1.call-start = ((), (), s32[]{:S(2)}) async-start(), calls=%async_computation.16 | async-start | bytes 7299072 | tf_op jit(solution)/shard_map/reduce_scatter | solution.py:297
  1050.8 4.9 copy-start.35
  1050.8 5.8 copy-start.22
  1050.8 5.8 copy-start.24
  (34 other events, 81.7 us)
Sparse Core Ops, SparseCore 0:
  9.6 72.8 all-gather.10
  90.1 44.0 all-gather.20
  136.7 45.5 all-gather.22
  184.0 72.1 all-gather.12
  257.6 30.4 all-gather.14
  289.5 88.5 all-gather.16
  379.6 87.8 all-gather.18
  819.7 61.9 reduce-scatter.13
  885.5 61.7 reduce-scatter.11
  952.4 96.9 reduce-scatter.23
  1055.3 97.9 reduce-scatter.17
  1160.6 134.5 reduce-scatter.19
  1301.6 134.6 reduce-scatter.21
  1443.3 118.1 reduce-scatter.15
